TPU v7x, 256 devices: a whole 4x4x8 slice. The times are simulated.
256 devices in a mesh: hid: 32 (over y, z), wid: 4 (over x), ad: 2 (over core).
Axes of the slice: x: 4, y: 4, z: 8, core: 2. Of those that a mesh axis runs over, the one named last changes fastest.
Arguments:
- activations: bfloat16 [1536, 2, 8192], P(None, None, ('wid', 'ad')), may hold values from -6 to 6
- row_adapter_index: int32 [1536, 2], replicated, may hold values from 0 to 127, as said below
- gate_up_weight: bfloat16 [8192, 2, 14848], P(('wid', 'ad'), None, 'hid'), may hold values from -0.0625 to 0.0625
- down_weight: bfloat16 [14848, 8192], P('hid', ('wid', 'ad')), may hold values from -0.046875 to 0.046875
- adapter_shrink_weight: bfloat16 [128, 2, 64, 8192], P(('hid', 'wid'), 'ad'), may hold values from -0.0625 to 0.0625
- adapter_expand_weight: bfloat16 [128, 2, 64, 14848], P(('hid', 'wid'), 'ad'), may hold values from -0.75 to 0.75
Outputs:
- layer_out: bfloat16 [1536, 2, 8192], P('hid', None, ('wid', 'ad'))
Inputs may be any that keep to these rules, and one draw needn't show every extreme that they name: `row_adapter_index`: call rows 48 * h to 48 * h + 47 of both batches together block h. In every block no adapter is named more than 2 times, and one and the same adapter is named exactly 2 times in every block.
All inputs are finite; a program needn't handle non-finite values.
Results may differ from a plain program's by a relative error of at most 0.0064.
Values may be sent and summed in bfloat16 or wider, within the bound.
No kernel may reach another device: no remote copies, remote signals or barrier semaphores. Data moves between devices by JAX's collectives and lax.ppermute only.
A program may use at most 128 MiB of HBM per device.

v0:
```python
import jax
import jax.numpy as jnp
from jax import lax
from jax.sharding import PartitionSpec as P


def slot_targets(block_ids, wid_count, wid_index, hid_count, group_capacity):
    row_count = block_ids.shape[1]
    matches = block_ids[:, :, None] == block_ids[:, None, :]
    earlier = jnp.arange(row_count)[None, :] < jnp.arange(row_count)[:, None]
    row_rank = jnp.sum(jnp.logical_and(matches, earlier[None]).astype(jnp.int32), axis=2)
    owner_hid = block_ids // wid_count
    is_mine = block_ids % wid_count == wid_index
    return jnp.where(is_mine, owner_hid * group_capacity + row_rank, hid_count * group_capacity)


def process_group(
    activations,
    row_adapter_index,
    gate_up_weight,
    down_weight,
    adapter_shrink_weight,
    adapter_expand_weight,
    group_capacity,
):
    hid_count = lax.axis_size("hid")
    wid_count = lax.axis_size("wid")
    hid_index = lax.axis_index("hid")
    wid_index = lax.axis_index("wid")
    proj_index = lax.axis_index("ad")
    total_rows, batch_count, local_width = activations.shape
    block_rows = total_rows // hid_count
    flat_width = block_rows * batch_count
    ff_local = down_weight.shape[0]
    own_rows = lax.dynamic_slice_in_dim(activations, hid_index * block_rows, block_rows, 0)
    full_rows = lax.all_gather(own_rows, ("wid", "ad"), axis=2, tiled=True)
    full_rows = full_rows.reshape(flat_width, -1)
    block_ids = row_adapter_index.reshape(hid_count, flat_width)
    targets = slot_targets(block_ids, wid_count, wid_index, hid_count, group_capacity)
    own_targets = lax.dynamic_index_in_dim(targets, hid_index, 0, keepdims=False)
    send_rows = jnp.zeros((hid_count * group_capacity, full_rows.shape[1]), full_rows.dtype)
    send_rows = (
        send_rows.at[own_targets].set(full_rows, mode="drop").reshape(hid_count, group_capacity, -1)
    )
    shrink_weight = adapter_shrink_weight[0, 0]
    expand_weight = adapter_expand_weight[0, 0]
    rank_values = jnp.einsum(
        "hcd,rd->hcr",
        lax.all_to_all(send_rows, "hid", split_axis=0, concat_axis=0, tiled=True),
        shrink_weight,
        preferred_element_type=jnp.float32,
    ).astype(jnp.bfloat16)
    deltas = jnp.einsum(
        "hcr,rf->hcf", rank_values, expand_weight, preferred_element_type=jnp.float32
    ).astype(jnp.bfloat16)
    deltas = deltas.reshape(hid_count, group_capacity, hid_count, ff_local)
    returned = lax.all_to_all(deltas, "hid", split_axis=2, concat_axis=2, tiled=True)
    row_slot = targets % group_capacity
    owner_slot = targets // group_capacity
    slot_total = hid_count * group_capacity * hid_count
    positions = (
        jnp.arange(hid_count, dtype=jnp.int32)[:, None] * group_capacity + row_slot
    ) * hid_count + owner_slot
    positions = jnp.where(targets < hid_count * group_capacity, positions, slot_total)
    flat_rows = (
        jnp.arange(hid_count, dtype=jnp.int32)[:, None] * flat_width
        + jnp.arange(flat_width, dtype=jnp.int32)[None, :]
    )
    slot_rows = jnp.full((slot_total,), total_rows * batch_count, jnp.int32)
    slot_rows = slot_rows.at[positions.reshape(-1)].set(flat_rows.reshape(-1), mode="drop")
    acts_flat = activations.reshape(total_rows * batch_count, local_width)
    weights = gate_up_weight.reshape(gate_up_weight.shape[0], -1)
    partial_value = jnp.dot(acts_flat, weights, preferred_element_type=jnp.float32).reshape(
        -1, 2, ff_local
    )
    partial_value = partial_value.at[slot_rows, proj_index].add(
        returned.reshape(-1, ff_local).astype(jnp.float32), mode="drop"
    )
    summed = lax.psum(partial_value, ("wid", "ad"))
    hidden = (jax.nn.silu(summed[:, 0]) * summed[:, 1]).astype(jnp.bfloat16)
    hidden_rows3 = hidden.reshape(total_rows, batch_count, ff_local)
    result = lax.psum_scatter(
        jnp.einsum("rbf,fd->rbd", hidden_rows3, down_weight, preferred_element_type=jnp.float32),
        "hid",
        scatter_dimension=0,
        tiled=True,
    )
    return result.astype(jnp.bfloat16)


def local(
    activations,
    row_adapter_index,
    gate_up_weight,
    down_weight,
    adapter_shrink_weight,
    adapter_expand_weight,
):
    hid_count = lax.axis_size("hid")
    wid_count = lax.axis_size("wid")
    block_rows = activations.shape[0] // hid_count
    batch_total = activations.shape[1]
    group_capacity = max(2, 2 * batch_total * block_rows // (hid_count * wid_count))
    return process_group(
        activations,
        row_adapter_index,
        gate_up_weight,
        down_weight,
        adapter_shrink_weight,
        adapter_expand_weight,
        group_capacity,
    )


def solution(mesh):
    in_specs = (
        P(None, None, ("wid", "ad")),
        P(),
        P(("wid", "ad"), None, "hid"),
        P("hid", ("wid", "ad")),
        P(("hid", "wid"), "ad", None, None),
        P(("hid", "wid"), "ad", None, None),
    )
    out_specs = P("hid", None, ("wid", "ad"))
    return jax.shard_map(local, mesh=mesh, in_specs=in_specs, out_specs=out_specs, check_vma=False)
```

profile of v0, /device:TPU:4, one launch (start us, length us, event | category | flops | bytes accessed | tf_op | source)
XLA Modules:
  0.0 711.8 jit_solution(1682355030441047729)
XLA Ops:
  11.1 28.2 %all-gather.2.cloned.1.call-done = bf16[48,2,8192]{2,1,0:T(2,128)(2,1)} async-done(((bf16[48,2,1024]{2,1,0:T(2,128)(2,1)}), bf16[48,2,8192]{2,1,0:T(2,128)(2,1)}) %all-gather.2.cloned.1.call-update) | async-done | bytes 1572880 | tf_op jit(solution)/shard_map/all_gather | solution.py:36
  39.3 3.7 reshape.318
  42.9 4.5 scatter_custom_fusion.1
  49.9 39.0 %all_to_all.10 = bf16[32,2,8192]{2,1,0:T(2,128)(2,1)} all-to-all(bf16[32,2,8192]{2,1,0:T(2,128)(2,1)} %reshape.299), channel_id=1, replica_groups=mesh['hid'=32,'wid'=4,'ad'=2] {'hid'}, dimensions={0} | all-to-all | bytes 2097152 | tf_op jit(solution)/shard_map/all_to_all | solution.py:49
  88.9 5.1 convolution_convert_fusion
  94.0 6.6 reshape.300
  100.6 5.0 copy.49
  105.7 5.3 all-to-all-start.1
  111.7 10.2 %reshape.328 = bf16[3072,1024,1]{1,0,2:T(8,128)(2,1)} reshape(bf16[1536,2,1024]{2,1,0:T(2,128)(2,1)} %param.6) | data formatting | bytes 12582912 | tf_op jit(solution)/shard_map/reshape | solution.py:71
  122.2 11.7 %fusion.5 = f32[3072,2,464]{0,2,1:T(8,128)} fusion(bf16[3072,1024,1]{1,0,2:T(8,128)(2,1)} %reshape.328, bf16[1024,2,464]{0,2,1:T(8,128)(2,1)S(1)} %copy-done), kind=kOutput, calls=%fused_computation.12 | convolution fusion | flops 5838471168 | bytes 19595264 | tf_op jit(solution)/shard_map/dot_general | solution.py:73
  134.0 18.8 %copy.45 = f32[3072,2,464]{2,1,0:T(2,128)} copy(f32[3072,2,464]{0,2,1:T(8,128)} %fusion.5) | data formatting | bytes 22806528 | tf_op jit(solution)/shard_map/dot_general | solution.py:73
  152.8 16.0 %reshape.302 = f32[6144,464]{1,0:T(8,128)} reshape(f32[3072,2,464]{2,1,0:T(2,128)} %copy.45) | data formatting | bytes 22806528
  169.0 11.8 %scatter_custom_fusion = s32[2048]{0:T(1024)S(1)} fusion(s32[3072]{0:T(1024)S(1)} %bitcast.37, s32[3072]{0:T(1024)S(1)} %reshape.310, s32[]{:T(128)} %constant.74.clone.1), kind=kCustom, calls=%fused_computation.45 | custom fusion | bytes 8196 | tf_op jit(solution)/shard_map/scatter | solution.py:70
  181.0 4.7 copy.50
  185.7 22.4 %scatter_custom_fusion.2 = f32[6144,464]{1,0:T(8,128)} fusion(f32[6144,464]{1,0:T(8,128)} %reshape.302, s32[2048]{0:T(1024)S(1)} %broadcast_select_fusion, bf16[2048,464]{1,0:T(8,128)(2,1)} %bitcast.34), kind=kCustom, calls=%fused_computation.7 | custom fusion | flops 1900544 | bytes 13500416
  208.1 15.5 %reshape.303 = f32[3072,2,464]{2,1,0:T(2,128)} reshape(f32[6144,464]{1,0:T(8,128)} %scatter_custom_fusion.2) | data formatting | bytes 22806528 | tf_op jit(solution)/shard_map/scatter-add | solution.py:76
  223.9 147.6 %all-reduce.3.cloned.1.call-done = f32[3072,2,464]{2,1,0:T(2,128)} async-done(((f32[3072,2,464]{2,1,0:T(2,128)}), f32[3072,2,464]{2,1,0:T(2,128)}) %all-reduce.3.cloned.1.call-update) | async-done | bytes 11403280 | tf_op jit(solution)/shard_map/psum | solution.py:79
  371.6 42.2 %slice_reduce_fusion.1 = (f32[3072,464]{1,0:T(8,128)}, f32[3072,464]{1,0:T(8,128)}) fusion(f32[3072,2,464]{2,1,0:T(2,128)} %all-reduce.3.cloned.1.call-done), kind=kLoop, calls=%fused_computation.5 | loop fusion | bytes 22806528 | tf_op jit(solution)/shard_map/slice | solution.py:80
  413.8 8.4 %squeeze.19 = f32[1536,2,464]{2,1,0:T(2,128)} reshape(f32[3072,464]{1,0:T(8,128)} %get-tuple-element.5) | data formatting | bytes 11403264 | tf_op jit(solution)/shard_map/squeeze | solution.py:80
  422.2 10.2 %copy.52 = f32[1536,2,464]{0,2,1:T(8,128)} copy(f32[1536,2,464]{2,1,0:T(2,128)} %squeeze.19) | data formatting | bytes 11403264 | tf_op jit(solution)/shard_map/squeeze | solution.py:80
  432.4 8.4 %squeeze.20 = f32[1536,2,464]{2,1,0:T(2,128)} reshape(f32[3072,464]{1,0:T(8,128)} %get-tuple-element.6) | data formatting | bytes 11403264 | tf_op jit(solution)/shard_map/squeeze | solution.py:80
  440.8 10.3 %copy.53 = f32[1536,2,464]{0,2,1:T(8,128)} copy(f32[1536,2,464]{2,1,0:T(2,128)} %squeeze.20) | data formatting | bytes 11403264 | tf_op jit(solution)/shard_map/squeeze | solution.py:80
  451.1 10.9 %fusion.2 = f32[1536,2,1024]{2,0,1:T(8,128)} fusion(f32[1536,2,464]{0,2,1:T(8,128)} %copy.53, f32[1536,2,464]{0,2,1:T(8,128)} %copy.52, bf16[464,1024]{1,0:T(8,128)(2,1)S(1)} %copy-done.4), kind=kOutput, calls=%fused_computation.9 | convolution fusion | flops 2927788032 | bytes 24936448 | tf_op jit(solution)/shard_map/rbf,fd->rbd/dot_general | solution.py:83
  462.1 241.3 %reduce-scatter.2.cloned.1.call-done = f32[48,2,1024]{2,0,1:T(8,128)} async-done(((f32[1536,2,1024]{2,0,1:T(8,128)}), f32[48,2,1024]{2,0,1:T(8,128)}) %reduce-scatter.2.cloned.1.call-update) | async-done | bytes 393232 | tf_op jit(solution)/shard_map/reduce_scatter | solution.py:82
  (41 shorter events, 10.7 us)
Async XLA Ops:
  6.5 115.7 %copy-start = (bf16[1024,2,464]{0,2,1:T(8,128)(2,1)S(1)}, bf16[1024,2,464]{0,2,1:T(8,128)(2,1)}, u32[]{:S(2)}) copy-start(bf16[1024,2,464]{0,2,1:T(8,128)(2,1)} %param.8) | copy-start | bytes 5701636
  6.5 32.7 %all-gather.2.cloned.1.call-start = ((), (), s32[]{:S(2)}) async-start(), calls=%async_computation.3 | async-start | bytes 1769472 | tf_op jit(solution)/shard_map/all_gather | solution.py:36
  105.7 75.3 %all-to-all-start.1 = ((bf16[32,2,32,464]{3,1,0,2:T(2,128)(2,1)}), bf16[32,2,32,464]{3,1,0,2:T(2,128)(2,1)}, u32[]{:S(2)}, u32[]{:S(2)}) async-start(bf16[32,2,32,464]{3,1,0,2:T(2,128)(2,1)} %copy.49), calls=%async_computation.1 | async-start | bytes 4194304 | tf_op jit(solution)/shard_map/all_to_all | solution.py:57
  110.9 260.6 %all-reduce.3.cloned.1.call-start = ((), (), s32[]{:S(2)}) async-start(), calls=%async_computation.4 | async-start | bytes 25165824 | tf_op jit(solution)/shard_map/psum | solution.py:79
  152.8 28.0 %copy-start.3 = (s32[2]{0:T(128)S(1)}, s32[2]{0:T(128)}, u32[]{:S(2)}) copy-start(s32[2]{0:T(128)} %constant.98) | copy-start | bytes 28
  152.8 28.1 %copy-start.2 = (s32[2]{0:T(128)S(1)}, s32[2]{0:T(128)}, u32[]{:S(2)}) copy-start(s32[2]{0:T(128)} %constant.101) | copy-start | bytes 28
  223.6 479.8 %reduce-scatter.2.cloned.1.call-start = ((), (), s32[]{:S(2)}) async-start(), calls=%async_computation.5 | async-start | bytes 12976128 | tf_op jit(solution)/shard_map/reduce_scatter | solution.py:82
  440.8 10.3 %copy-start.4 = (bf16[464,1024]{1,0:T(8,128)(2,1)S(1)}, bf16[464,1024]{1,0:T(8,128)(2,1)}, u32[]{:S(2)}) copy-start(bf16[464,1024]{1,0:T(8,128)(2,1)} %param.9) | copy-start | bytes 2850820
  462.0 243.3 %copy-start.1 = (bf16[1024,2,464]{0,2,1:T(8,128)(2,1)S(1)}, bf16[1024,2,464]{0,2,1:T(8,128)(2,1)}, u32[]{:S(2)}) copy-start(bf16[1024,2,464]{0,2,1:T(8,128)(2,1)} %param.8) | copy-start | bytes 5701636
Sparse Core Ops, SparseCore 0:
  9.2 30.0 all-gather.1
  223.8 147.7 all-reduce.2
  462.2 241.1 reduce-scatter.1
where the time goes:
time: 715 us; the launch traced here: 712 us
  waiting for transfers between devices  417 us (58%)
  local copies, waits for them, and re-layouts  184 us (26%)
  blocking collectives  39 us (5%)
  matrix products  27.8 us (4%)
  other arithmetic  25.2 us (4%)
  between operations  13.3 us (2%)
    reduce_scatter x1, waiting for transfers between devices, process_group(): lax.psum_scatter(jnp.einsum('rbf,fd->rbd', hidden_rows3, down_weight, pre...  241 us
    psum x1, waiting for transfers between devices, process_group(): summed = lax.psum(partial_value, ('wid', 'ad'))  148 us
    slice x1, local copies, waits for them, and re-layouts, process_group(): hidden = (jax.nn.silu(summed[:, 0]) * summed[:, 1]).astype(jnp.bfloat16)  42.2 us
    all_to_all x1, blocking collectives, process_group(): lax.all_to_all(send_rows, 'hid', split_axis=0, concat_axis=0, tiled=True)  39 us
    squeeze x4, local copies, waits for them, and re-layouts, process_group(): hidden = (jax.nn.silu(summed[:, 0]) * summed[:, 1]).astype(jnp.bfloat16)  37.3 us
    all_gather x1, waiting for transfers between devices, process_group(): full_rows = lax.all_gather(own_rows, ('wid', 'ad'), axis=2, tiled=True)  28.2 us
    unnamed x4, other arithmetic  22.6 us
    dot_general x1, local copies, waits for them, and re-layouts, process_group(): jnp.dot(acts_flat, weights, preferred_element_type=jnp.float32)  18.8 us
  transfers between devices with their start and end apart: 4, of which 3 were waited for; matrix products, arithmetic and copies ran while one was open for 10% of the time, Pallas kernels for 0%

commit v1 on v0

--- a/solution.py
+++ b/solution.py
@@ -2,6 +2,10 @@
 import jax.numpy as jnp
 from jax import lax
 from jax.sharding import PartitionSpec as P
+
+
+def carry_the_scenes(view, along_axis):
+    return jnp.sum(lax.all_gather(view, along_axis), axis=0)
 
 
 def slot_targets(block_ids, wid_count, wid_index, hid_count, group_capacity):
@@ -76,7 +80,7 @@
     partial_value = partial_value.at[slot_rows, proj_index].add(
         returned.reshape(-1, ff_local).astype(jnp.float32), mode="drop"
     )
-    summed = lax.psum(partial_value, ("wid", "ad"))
+    summed = carry_the_scenes(partial_value, ("wid", "ad"))
     hidden = (jax.nn.silu(summed[:, 0]) * summed[:, 1]).astype(jnp.bfloat16)
     hidden_rows3 = hidden.reshape(total_rows, batch_count, ff_local)
     result = lax.psum_scatter(

time: 715 us -> 1000 us (1.40)
  waiting for transfers between devices: 417 us -> 669 us
  other arithmetic: 25.2 us -> 58.2 us
    all_gather x0 -> x1, waiting for transfers between devices: none -> 400 us  [carry_the_scenes(): return jnp.sum(lax.all_gather(view, along_axis), axis=0)]
    psum x1 -> x0, waiting for transfers between devices: 148 us -> none  [process_group(): summed = lax.psum(partial_value, ('wid', 'ad'))]
    all_gather x0 -> x2, local copies, waits for them, and re-layouts: none -> 34.5 us  [carry_the_scenes(): return jnp.sum(lax.all_gather(view, along_axis), axis=0)]
    reduce_sum x0 -> x1, other arithmetic: none -> 33 us  [carry_the_scenes(): return jnp.sum(lax.all_gather(view, along_axis), axis=0)]
    slice x1, local copies, waits for them, and re-layouts: 42.2 us -> 9.92 us  [process_group(): hidden = (jax.nn.silu(summed[:, 0]) * summed[:, 1]).astype(jnp.bfloat16)]
    scatter-add x1 -> x0, local copies, waits for them, and re-layouts: 15.5 us -> none  [process_group(): partial_value.at[slot_rows, proj_index]]
    unnamed x12 -> x14, local copies, waits for them, and re-layouts: 17 us -> 29.8 us
  transfers between devices with their start and end apart: 4 -> 4, of which waited for: 3 -> 3; matrix products, arithmetic and copies ran while one was open for 10% -> 7% of each run, Pallas kernels for 0% -> 0%
where the time goes in v1:
time: 1000 us; the launch traced here: 996 us
  waiting for transfers between devices  669 us (67%)
  local copies, waits for them, and re-layouts  183 us (18%)
  other arithmetic  58.2 us (6%)
  blocking collectives  39 us (4%)
  matrix products  27.8 us (3%)
  between operations  13.3 us (1%)
    all_gather x1, waiting for transfers between devices, carry_the_scenes(): return jnp.sum(lax.all_gather(view, along_axis), axis=0)  400 us
    reduce_scatter x1, waiting for transfers between devices, process_group(): lax.psum_scatter(jnp.einsum('rbf,fd->rbd', hidden_rows3, down_weight, pre...  241 us
    all_to_all x1, blocking collectives, process_group(): lax.all_to_all(send_rows, 'hid', split_axis=0, concat_axis=0, tiled=True)  39 us
    squeeze x4, local copies, waits for them, and re-layouts, process_group(): hidden = (jax.nn.silu(summed[:, 0]) * summed[:, 1]).astype(jnp.bfloat16)  37.2 us
    all_gather x2, local copies, waits for them, and re-layouts, carry_the_scenes(): return jnp.sum(lax.all_gather(view, along_axis), axis=0)  34.5 us
    reduce_sum x1, other arithmetic, carry_the_scenes(): return jnp.sum(lax.all_gather(view, along_axis), axis=0)  33 us
    unnamed x14, local copies, waits for them, and re-layouts  29.8 us
    all_gather x1, waiting for transfers between devices, process_group(): full_rows = lax.all_gather(own_rows, ('wid', 'ad'), axis=2, tiled=True)  28.2 us
  transfers between devices with their start and end apart: 4, of which 3 were waited for; matrix products, arithmetic and copies ran while one was open for 7% of the time, Pallas kernels for 0%

profile of v1, /device:TPU:4, one launch (start us, length us, event | category | flops | bytes accessed | tf_op | source)
XLA Modules:
  0.0 996.1 jit_solution(4449954403367666932)
XLA Ops:
  11.1 28.2 %all-gather.3.cloned.1.call-done = bf16[48,2,8192]{2,1,0:T(2,128)(2,1)} async-done(((bf16[48,2,1024]{2,1,0:T(2,128)(2,1)}), bf16[48,2,8192]{2,1,0:T(2,128)(2,1)}) %all-gather.3.cloned.1.call-update) | async-done | bytes 1572880 | tf_op jit(solution)/shard_map/all_gather | solution.py:40
  49.9 39.0 %all_to_all.10 = bf16[32,2,8192]{2,1,0:T(2,128)(2,1)} all-to-all(bf16[32,2,8192]{2,1,0:T(2,128)(2,1)} %reshape.299), channel_id=1, replica_groups=mesh['hid'=32,'wid'=4,'ad'=2] {'hid'}, dimensions={0} | all-to-all | bytes 2097152 | tf_op jit(solution)/shard_map/all_to_all | solution.py:53
  88.9 5.1 convolution_convert_fusion
  94.0 6.6 reshape.300
  105.7 5.3 all-to-all-start.1
  111.7 10.2 %reshape.329 = bf16[3072,1024,1]{1,0,2:T(8,128)(2,1)} reshape(bf16[1536,2,1024]{2,1,0:T(2,128)(2,1)} %param.6) | data formatting | bytes 12582912 | tf_op jit(solution)/shard_map/reshape | solution.py:75
  122.2 11.7 %fusion.5 = f32[3072,2,464]{0,2,1:T(8,128)} fusion(bf16[3072,1024,1]{1,0,2:T(8,128)(2,1)} %reshape.329, bf16[1024,2,464]{0,2,1:T(8,128)(2,1)S(1)} %copy-done), kind=kOutput, calls=%fused_computation.12 | convolution fusion | flops 5838471168 | bytes 19595264 | tf_op jit(solution)/shard_map/dot_general | solution.py:77
  134.0 18.8 %copy.53 = f32[3072,2,464]{2,1,0:T(2,128)} copy(f32[3072,2,464]{0,2,1:T(8,128)} %fusion.5) | data formatting | bytes 22806528 | tf_op jit(solution)/shard_map/dot_general | solution.py:77
  152.8 16.0 %reshape.302 = f32[6144,464]{1,0:T(8,128)} reshape(f32[3072,2,464]{2,1,0:T(2,128)} %copy.53) | data formatting | bytes 22806528
  169.0 11.8 %scatter_custom_fusion = s32[2048]{0:T(1024)S(1)} fusion(s32[3072]{0:T(1024)S(1)} %bitcast.41, s32[3072]{0:T(1024)S(1)} %reshape.311, s32[]{:T(128)} %constant.75.clone.1), kind=kCustom, calls=%fused_computation.45 | custom fusion | bytes 8196 | tf_op jit(solution)/shard_map/scatter | solution.py:74
  185.7 22.4 %scatter_custom_fusion.2 = f32[6144,464]{1,0:T(8,128)} fusion(f32[6144,464]{1,0:T(8,128)} %reshape.302, s32[2048]{0:T(1024)S(1)} %broadcast_select_fusion, bf16[2048,464]{1,0:T(8,128)(2,1)} %bitcast.38), kind=kCustom, calls=%fused_computation.7 | custom fusion | flops 1900544 | bytes 13500416
  208.1 15.5 %all_gather.10 = f32[1,3072,2,464]{3,2,1,0:T(2,128)} reshape(f32[6144,464]{1,0:T(8,128)} %scatter_custom_fusion.2) | data formatting | bytes 22806528 | tf_op jit(solution)/shard_map/all_gather | solution.py:8
  223.6 19.0 %copy.59 = f32[1,3072,2,464]{1,3,2,0:T(8,128)} copy(f32[1,3072,2,464]{3,2,1,0:T(2,128)} %all_gather.10) | data formatting | bytes 22806528 | tf_op jit(solution)/shard_map/all_gather | solution.py:8
  242.9 400.2 %all-gather.5.cloned.1.call-done = f32[8,3072,2,464]{1,3,2,0:T(8,128)} async-done(((f32[1,3072,2,464]{1,3,2,0:T(8,128)}), f32[8,3072,2,464]{1,3,2,0:T(8,128)}) %all-gather.5.cloned.1.call-update) | async-done | bytes 91226128 | tf_op jit(solution)/shard_map/all_gather | solution.py:8
  643.1 33.0 %reduce_sum.22 = f32[3072,2,464]{0,2,1:T(8,128)} reduce(f32[8,3072,2,464]{1,3,2,0:T(8,128)} %all-gather.5.cloned.1.call-done, f32[]{:T(128)} %constant.92.clone.1), dimensions={0}, to_apply=%region_4.5 | reduce | flops 19955712 | bytes 102629376 | tf_op jit(solution)/shard_map/reduce_sum | solution.py:8
  676.1 9.9 slice_bitcast_fusion.1
  686.1 6.4 copy.72
  692.5 8.4 squeeze.19
  700.9 10.2 %copy.62 = f32[1536,2,464]{0,2,1:T(8,128)} copy(f32[1536,2,464]{2,1,0:T(2,128)} %squeeze.19) | data formatting | bytes 11403264 | tf_op jit(solution)/shard_map/squeeze | solution.py:84
  711.0 6.4 copy.73
  717.4 8.4 squeeze.20
  725.8 10.3 %copy.63 = f32[1536,2,464]{0,2,1:T(8,128)} copy(f32[1536,2,464]{2,1,0:T(2,128)} %squeeze.20) | data formatting | bytes 11403264 | tf_op jit(solution)/shard_map/squeeze | solution.py:84
  736.1 10.9 %fusion.2 = f32[1536,2,1024]{2,0,1:T(8,128)} fusion(f32[1536,2,464]{0,2,1:T(8,128)} %copy.63, f32[1536,2,464]{0,2,1:T(8,128)} %copy.62, bf16[464,1024]{1,0:T(8,128)(2,1)S(1)} %copy-done.4), kind=kOutput, calls=%fused_computation.9 | convolution fusion | flops 2927788032 | bytes 24936448 | tf_op jit(solution)/shard_map/rbf,fd->rbd/dot_general | solution.py:87
  747.1 240.6 %reduce-scatter.2.cloned.1.call-done = f32[48,2,1024]{2,0,1:T(8,128)} async-done(((f32[1536,2,1024]{2,0,1:T(8,128)}), f32[48,2,1024]{2,0,1:T(8,128)}) %reduce-scatter.2.cloned.1.call-update) | async-done | bytes 393232 | tf_op jit(solution)/shard_map/reduce_scatter | solution.py:86
  (45 shorter events, 28.6 us)
Async XLA Ops:
  6.5 115.7 %copy-start = (bf16[1024,2,464]{0,2,1:T(8,128)(2,1)S(1)}, bf16[1024,2,464]{0,2,1:T(8,128)(2,1)}, u32[]{:S(2)}) copy-start(bf16[1024,2,464]{0,2,1:T(8,128)(2,1)} %param.8) | copy-start | bytes 5701636
  6.5 32.7 %all-gather.3.cloned.1.call-start = ((), (), s32[]{:S(2)}) async-start(), calls=%async_computation.3 | async-start | bytes 1769472 | tf_op jit(solution)/shard_map/all_gather | solution.py:40
  105.7 75.3 %all-to-all-start.1 = ((bf16[32,2,32,464]{3,1,0,2:T(2,128)(2,1)}), bf16[32,2,32,464]{3,1,0,2:T(2,128)(2,1)}, u32[]{:S(2)}, u32[]{:S(2)}) async-start(bf16[32,2,32,464]{3,1,0,2:T(2,128)(2,1)} %copy.57), calls=%async_computation.1 | async-start | bytes 4194304 | tf_op jit(solution)/shard_map/all_to_all | solution.py:61
  110.9 532.2 %all-gather.5.cloned.1.call-start = ((), (), s32[]{:S(2)}) async-start(), calls=%async_computation.4 | async-start | bytes 102629376 | tf_op jit(solution)/shard_map/all_gather | solution.py:8
  152.8 28.0 %copy-start.3 = (s32[2]{0:T(128)S(1)}, s32[2]{0:T(128)}, u32[]{:S(2)}) copy-start(s32[2]{0:T(128)} %constant.100) | copy-start | bytes 28
  152.8 28.1 %copy-start.2 = (s32[2]{0:T(128)S(1)}, s32[2]{0:T(128)}, u32[]{:S(2)}) copy-start(s32[2]{0:T(128)} %constant.103) | copy-start | bytes 28
  242.6 745.1 %reduce-scatter.2.cloned.1.call-start = ((), (), s32[]{:S(2)}) async-start(), calls=%async_computation.5 | async-start | bytes 12976128 | tf_op jit(solution)/shard_map/reduce_scatter | solution.py:86
  725.8 10.3 %copy-start.4 = (bf16[464,1024]{1,0:T(8,128)(2,1)S(1)}, bf16[464,1024]{1,0:T(8,128)(2,1)}, u32[]{:S(2)}) copy-start(bf16[464,1024]{1,0:T(8,128)(2,1)} %param.9) | copy-start | bytes 2850820
  747.0 242.5 %copy-start.1 = (bf16[1024,2,464]{0,2,1:T(8,128)(2,1)S(1)}, bf16[1024,2,464]{0,2,1:T(8,128)(2,1)}, u32[]{:S(2)}) copy-start(bf16[1024,2,464]{0,2,1:T(8,128)(2,1)} %param.8) | copy-start | bytes 5701636
Sparse Core Ops, SparseCore 0:
  9.2 30.0 all-gather.2
  242.7 400.3 all-gather.4
  747.2 240.4 reduce-scatter.1
